TPU v7x, 32 devices: a whole 2x2x4 slice. The times are simulated.
32 devices in a mesh: row: 2 (over core), col: 4 (over z), ind: 4 (over y, x).
Axes of the slice: x: 2, y: 2, z: 4, core: 2. Of those that a mesh axis runs over, the one named last changes fastest.
Arguments:
- dosages: bfloat16 [4096, 1024], P('ind', ('row', 'col'))
- annotations: bfloat16 [1024, 1024], P('ind', ('row', 'col')), may hold values from -6 to 6
- window_end: int32 [1024], P(('row', 'col')), may hold values from 512 to 1024, as said below
Outputs:
- ld_scores: float32 [1024, 1024], P('ind', ('row', 'col'))
Inputs may be any that keep to these rules, and one draw needn't show every extreme that they name: window_end is nondecreasing, window_end[j] > j, and window_end[j] <= min(1024, (j // 128 + 4) * 128), the last bound reached in every draw.
All inputs are finite; a program needn't handle non-finite values.
Results may differ from a plain program's by a relative error of at most 0.0029.
Values may be sent and summed in bfloat16 or wider, within the bound.
A program may use at most 64 MiB of HBM per device.

v0:
```python
import jax
import jax.numpy as jnp
from jax import lax
from jax.sharding import PartitionSpec as P


def from_behind(array, axis, by):
    count = lax.axis_size(axis)
    pairs = [(i, i + by) for i in range(count) if 0 <= i + by < count]
    return lax.ppermute(array, axis, pairs)


def per_device(dosages, annotations, window_end):
    band_count = lax.axis_size("col")
    column_index = lax.axis_index("col")
    tile_size = dosages.shape[1]
    ind_rows = dosages.shape[0]
    ann_rows = annotations.shape[0]
    group_width = band_count * tile_size
    sample_count = ind_rows * lax.axis_size("ind")
    window_ends = lax.all_gather(window_end, "col", axis=0, tiled=True)
    group_x, group_a = (
        lax.all_gather(dosages, "col", axis=1, tiled=True),
        lax.all_gather(annotations, "col", axis=1, tiled=True),
    )
    next_x, next_a = from_behind((group_x, group_a), "row", -1)
    wide_x = jnp.concatenate([group_x, next_x], axis=1)
    wide_a = jnp.concatenate([group_a, next_a], axis=1)
    band_x = lax.dynamic_slice_in_dim(wide_x, column_index * tile_size, group_width, 1)
    band_a = lax.dynamic_slice_in_dim(wide_a, column_index * tile_size, group_width, 1)
    rows_x = group_x.reshape(ind_rows, band_count, tile_size)
    cols_x = band_x.reshape(ind_rows, band_count, tile_size)
    partial_gram = jnp.einsum("inb,ine->nbe", rows_x, cols_x, preferred_element_type=jnp.float32)
    gram = lax.psum(partial_gram, "ind")
    correlation_matrix = gram / sample_count
    raw_rsquared = correlation_matrix * correlation_matrix
    unbiased_rsquared = raw_rsquared - (1.0 - raw_rsquared) / (sample_count - 2)
    group_start = lax.axis_index("row") * group_width
    block_ids = jnp.arange(band_count, dtype=jnp.int32)[:, None, None]
    within_window = jnp.arange(tile_size, dtype=jnp.int32)
    row_pos = group_start + block_ids * tile_size + within_window[None, :, None]
    col_pos = group_start + (block_ids + column_index) * tile_size + within_window[None, None, :]
    limit = window_ends.reshape(band_count, tile_size)[:, :, None]
    inside = col_pos < limit
    upper = jnp.where((col_pos >= row_pos) & inside, unbiased_rsquared, 0.0).astype(jnp.bfloat16)
    strict = jnp.where((col_pos > row_pos) & inside, unbiased_rsquared, 0.0).astype(jnp.bfloat16)
    annotation_rows = group_a.reshape(ann_rows, band_count, tile_size)
    cols_a = band_a.reshape(ann_rows, band_count, tile_size)
    direct = jnp.einsum("cne,nae->cna", cols_a, upper, preferred_element_type=jnp.float32)
    mirror = jnp.einsum("cna,nae->cne", annotation_rows, strict, preferred_element_type=jnp.float32)
    direct = direct.reshape(ann_rows, group_width)
    mirror = mirror.reshape(ann_rows, group_width)
    window_acc = jnp.zeros((ann_rows, 2 * group_width), jnp.float32)
    window_acc = lax.dynamic_update_slice_in_dim(window_acc, mirror, column_index * tile_size, 1)
    window_acc = window_acc.at[:, :group_width].add(direct)
    incoming = from_behind(window_acc[:, group_width:], "row", 1)
    combined = window_acc[:, :group_width] + incoming
    ld_scores = lax.psum_scatter(combined, "col", scatter_dimension=1, tiled=True)
    return ld_scores


def solution(mesh):
    in_specs = (P("ind", ("row", "col")), P("ind", ("row", "col")), P(("row", "col")))
    out_specs = P("ind", ("row", "col"))
    return jax.shard_map(
        per_device, mesh=mesh, in_specs=in_specs, out_specs=out_specs, check_vma=False
    )
```

profile of v0, /device:TPU:0, one launch (start us, length us, event | category | flops | bytes accessed | tf_op | source)
XLA Modules:
  0.0 139.3 jit_solution(7500563988074717324)
XLA Ops:
  6.5 1.8 %copy.16 = bf16[1024,128]{0,1:T(8,128)(2,1)} copy(bf16[1024,128]{1,0:T(8,128)(2,1)} %param.5) | data formatting | bytes 524288 | tf_op args[0]
  8.3 0.0 all-gather.3.cloned.1.call-update
  8.4 0.0 all-reduce.2.cloned.1.call-start
  8.4 31.2 %all-gather.3.cloned.1.call-done = bf16[1024,512]{0,1:T(8,128)(2,1)} async-done(((bf16[1024,128]{0,1:T(8,128)(2,1)}), bf16[1024,512]{0,1:T(8,128)(2,1)}) %all-gather.3.cloned.1.call-update) | async-done | bytes 1048592 | tf_op jit(solution)/shard_map/all_gather | solution.py:23
  39.6 1.3 collective-permute-start
  40.9 0.9 copy.18
  41.9 14.4 %all_gather.11 = bf16[256,512]{0,1:T(8,128)(2,1)S(1)} all-gather(bf16[256,128]{0,1:T(8,128)(2,1)S(1)} %copy.18), channel_id=1, replica_groups=mesh['row'=2,'col'=4,'ind'=4] {'col'}, dimensions={1}, use_global_device_ids=true | all-gather | bytes 327680 | tf_op jit(solution)/shard_map/all_gather | solution.py:24
  56.2 1.3 collective-permute-start.1
  57.6 0.0 collective-permute-done
  57.6 2.3 %fusion = bf16[1024,512]{0,1:T(8,128)(2,1)S(1)} fusion(s32[]{:T(128)S(6)} %select_n.12, bf16[1024,512]{0,1:T(8,128)(2,1)} %all-gather.3.cloned.1.call-done, bf16[1024,512]{0,1:T(8,128)(2,1)S(1)} %collective-permute-done), kind=kLoop, calls=%fused_computation.3 | loop fusion | flops 2097152 | bytes 3145732 | tf_op jit(solution)/shard_map/concatenate | solution.py:27
  59.9 0.0 copy-start.2
  59.9 1.1 convolution_bitcast_fusion
  61.0 0.0 all-reduce.2.cloned.1.call-update
  61.1 0.0 reduce-scatter.2.cloned.1.call-start
  61.1 0.1 iota_add_fusion
  61.2 9.1 %all-gather = s32[4,1,128]{2,1,0:T(1,128)S(1)} all-gather(s32[1,1,128]{2,1,0:T(1,128)S(1)} %bitcast.26), channel_id=1, replica_groups=mesh['row'=2,'col'=4,'ind'=4] {'col'}, dimensions={0}, use_global_device_ids=true | all-gather | bytes 2560 | tf_op jit(solution)/shard_map/all_gather | solution.py:21
  70.3 0.1 iota_add_fusion.1
  70.3 33.8 %all-reduce.2.cloned.1.call-done = f32[4,128,128]{1,2,0:T(8,128)} async-done(((f32[4,128,128]{1,2,0:T(8,128)}), f32[4,128,128]{1,2,0:T(8,128)}) %all-reduce.2.cloned.1.call-update) | async-done | bytes 262160 | tf_op jit(solution)/shard_map/psum | solution.py:34
  104.2 1.2 fusion.3
  105.4 0.2 copy.20
  105.6 0.1 broadcast_in_dim.11
  105.7 0.1 constant_dynamic-update-slice_fusion
  105.8 1.5 %collective-permute-start.2 = (f32[256,512]{1,0:T(8,128)S(1)}, f32[256,512]{1,0:T(8,128)S(1)}, u32[]{:S(2)}, u32[]{:S(2)}) collective-permute-start(f32[256,512]{1,0:T(8,128)S(1)} %slice.29), channel_id=1, source_target_pairs={{0,16},{1,17},{2,18},{3,19},{4,20},{5,21},{6,22},{7,23},{8,24},{9,... | collective-permute-start | bytes 1572872 | tf_op jit(solution)/shard_map/ppermute | solution.py:10
  107.3 0.6 compare_reduce_fusion
  107.9 0.0 collective-permute-done.1
  107.9 0.6 fusion.2
  108.6 0.4 fusion.4
  108.9 0.2 copy.23
  109.1 0.0 collective-permute-done.2
  109.1 1.6 %fusion.1 = f32[256,512]{1,0:T(8,128)} fusion(f32[256,512]{1,0:T(8,128)S(1)} %collective-permute-done.2, f32[256,512]{1,0:T(8,128)S(1)} %copy.23, f32[256,1024]{1,0:T(8,128)S(1)} %constant_dynamic-update-slice_fusion, pred[]{:T(512)} %compare_reduce_fusion), kind=kLoop, calls=%fused_computation.5 | loop fusion | flops 393216 | bytes 2097153 | tf_op jit(solution)/shard_map/add | solution.py:57
  110.7 0.0 reduce-scatter.2.cloned.1.call-update
  110.8 22.0 %reduce-scatter.2.cloned.1.call-done = f32[256,128]{1,0:T(8,128)} async-done(((f32[256,512]{1,0:T(8,128)}), f32[256,128]{1,0:T(8,128)}) %reduce-scatter.2.cloned.1.call-update) | async-done | bytes 131088 | tf_op jit(solution)/shard_map/reduce_scatter | solution.py:58
  (8 shorter events, 0.1 us)
Async XLA Ops:
  6.5 33.1 %all-gather.3.cloned.1.call-start = ((), (), s32[]{:S(2)}) async-start(), calls=%async_computation.1 | async-start | bytes 1310720 | tf_op jit(solution)/shard_map/all_gather | solution.py:23
  8.4 95.8 %all-reduce.2.cloned.1.call-start = ((), (), s32[]{:S(2)}) async-start(), calls=%async_computation.2 | async-start | bytes 524288 | tf_op jit(solution)/shard_map/psum | solution.py:34
  39.6 17.9 %collective-permute-start = (bf16[1024,512]{0,1:T(8,128)(2,1)}, bf16[1024,512]{0,1:T(8,128)(2,1)S(1)}, u32[]{:S(2)}, u32[]{:S(2)}) collective-permute-start(bf16[1024,512]{0,1:T(8,128)(2,1)} %all-gather.3.cloned.1.call-done), channel_id=1, source_target_pairs={{16,0},{17,1},{18,2},{19,3},{20,4},{21,5},{22,6},{23,7},{24,8},{25... | collective-permute-start | bytes 3145736 | tf_op jit(solution)/shard_map/ppermute | solution.py:10
  56.2 51.7 %collective-permute-start.1 = (bf16[256,512]{0,1:T(8,128)(2,1)S(1)}, bf16[256,512]{0,1:T(8,128)(2,1)S(1)}, u32[]{:S(2)}, u32[]{:S(2)}) collective-permute-start(bf16[256,512]{0,1:T(8,128)(2,1)S(1)} %all_gather.11), channel_id=1, source_target_pairs={{16,0},{17,1},{18,2},{19,3},{20,4},{21,5},{22,6},{23,7},{24,8},{25... | collective-permute-start | bytes 786440 | tf_op jit(solution)/shard_map/ppermute | solution.py:10
  57.6 2.3 %copy-start = (bf16[1024,512]{0,1:T(8,128)(2,1)S(1)}, bf16[1024,512]{0,1:T(8,128)(2,1)}, u32[]{:S(2)}) copy-start(bf16[1024,512]{0,1:T(8,128)(2,1)} %all-gather.3.cloned.1.call-done) | copy-start | bytes 3145732
  59.9 1.3 copy-start.2
  61.1 71.7 %reduce-scatter.2.cloned.1.call-start = ((), (), s32[]{:S(2)}) async-start(), calls=%async_computation.3 | async-start | bytes 655360 | tf_op jit(solution)/shard_map/reduce_scatter | solution.py:58
  105.8 2.8 %copy-start.1 = (f32[4,128,128]{1,2,0:T(8,128)S(1)}, f32[4,128,128]{1,2,0:T(8,128)}, u32[]{:S(2)}) copy-start(f32[4,128,128]{1,2,0:T(8,128)} %all-reduce.2.cloned.1.call-done) | copy-start | bytes 786436
  105.8 3.3 %collective-permute-start.2 = (f32[256,512]{1,0:T(8,128)S(1)}, f32[256,512]{1,0:T(8,128)S(1)}, u32[]{:S(2)}, u32[]{:S(2)}) collective-permute-start(f32[256,512]{1,0:T(8,128)S(1)} %slice.29), channel_id=1, source_target_pairs={{0,16},{1,17},{2,18},{3,19},{4,20},{5,21},{6,22},{7,23},{8,24},{9,... | collective-permute-start | bytes 1572872 | tf_op jit(solution)/shard_map/ppermute | solution.py:10
Sparse Core Ops, SparseCore 0:
  8.9 30.6 all-gather.2
  61.2 42.9 all-reduce.1
  110.9 21.8 reduce-scatter.1
where the time goes:
time: 140 us; the launch traced here: 139 us
  waiting for transfers between devices  87.1 us (62%)
  blocking collectives  23.5 us (17%)
  between operations  13.3 us (10%)
  other arithmetic  5.3 us (4%)
  starting transfers between devices  4.1 us (3%)
  local copies, waits for them, and re-layouts  3.35 us (2%)
  matrix products  2.71 us (2%)
    psum x1, waiting for transfers between devices, per_device(): gram = lax.psum(partial_gram, 'ind')  33.8 us
    all_gather x1, waiting for transfers between devices, per_device(): lax.all_gather(dosages, 'col', axis=1, tiled=True)  31.2 us
    reduce_scatter x1, waiting for transfers between devices, per_device(): lax.psum_scatter(combined, 'col', scatter_dimension=1, tiled=True)  22 us
    all_gather x1, blocking collectives, per_device(): lax.all_gather(annotations, 'col', axis=1, tiled=True)  14.4 us
    all_gather x1, blocking collectives, per_device(): window_ends = lax.all_gather(window_end, 'col', axis=0, tiled=True)  9.09 us
    ppermute x3, starting transfers between devices, from_behind(): return lax.ppermute(array, axis, pairs)  4.02 us
  transfers between devices with their start and end apart: 6, of which 3 were waited for; matrix products, arithmetic and copies ran while one was open for 6% of the time, Pallas kernels for 0%

commit v1 on v0

--- a/solution.py
+++ b/solution.py
@@ -31,7 +31,7 @@
     rows_x = group_x.reshape(ind_rows, band_count, tile_size)
     cols_x = band_x.reshape(ind_rows, band_count, tile_size)
     partial_gram = jnp.einsum("inb,ine->nbe", rows_x, cols_x, preferred_element_type=jnp.float32)
-    gram = lax.psum(partial_gram, "ind")
+    gram = jnp.sum(lax.all_gather(partial_gram, "ind"), axis=0)
     correlation_matrix = gram / sample_count
     raw_rsquared = correlation_matrix * correlation_matrix
     unbiased_rsquared = raw_rsquared - (1.0 - raw_rsquared) / (sample_count - 2)

time: 140 us -> 110 us (0.79)
  waiting for transfers between devices: 87.1 us -> 57.9 us
  matrix products: 2.71 us -> 1.06 us
    psum x1 -> x0, waiting for transfers between devices: 33.8 us -> none  [per_device(): gram = lax.psum(partial_gram, 'ind')]
    ppermute x3, waiting for transfers between devices: 0.01 us -> 3.45 us  [from_behind(): return lax.ppermute(array, axis, pairs)]
  transfers between devices with their start and end apart: 6 -> 6, of which waited for: 3 -> 4; matrix products, arithmetic and copies ran while one was open for 6% -> 4% of each run, Pallas kernels for 0% -> 0%
where the time goes in v1:
time: 110 us
  waiting for transfers between devices  57.9 us (53%)
  blocking collectives  23 us (21%)
  between operations  13.3 us (12%)
  other arithmetic  6.51 us (6%)
  starting transfers between devices  4.25 us (4%)
  local copies, waits for them, and re-layouts  3.48 us (3%)
    all_gather x1, waiting for transfers between devices, per_device(): lax.all_gather(dosages, 'col', axis=1, tiled=True)  31.2 us
    reduce_scatter x1, waiting for transfers between devices, per_device(): lax.psum_scatter(combined, 'col', scatter_dimension=1, tiled=True)  22 us
    all_gather x1, blocking collectives, per_device(): lax.all_gather(annotations, 'col', axis=1, tiled=True)  13.9 us
    all_gather x1, blocking collectives, per_device(): window_ends = lax.all_gather(window_end, 'col', axis=0, tiled=True)  9.16 us
    ppermute x3, starting transfers between devices, from_behind(): return lax.ppermute(array, axis, pairs)  4.17 us
    ppermute x3, waiting for transfers between devices, from_behind(): return lax.ppermute(array, axis, pairs)  3.45 us
    concatenate x1, other arithmetic, per_device(): wide_x = jnp.concatenate([group_x, next_x], axis=1)  2.21 us
  transfers between devices with their start and end apart: 6, of which 4 were waited for; matrix products, arithmetic and copies ran while one was open for 4% of the time, Pallas kernels for 0%

profile of v1, /device:TPU:0, one launch (start us, length us, event | category | flops | bytes accessed | tf_op | source)
XLA Modules:
  0.0 109.5 jit_solution(13344527033893841829)
XLA Ops:
  6.5 1.8 %copy.16 = bf16[1024,128]{0,1:T(8,128)(2,1)} copy(bf16[1024,128]{1,0:T(8,128)(2,1)} %param.5) | data formatting | bytes 524288 | tf_op args[0]
  8.3 0.0 all-gather.5.cloned.1.call-update
  8.4 0.0 all-gather.7.cloned.1.call-start
  8.4 31.2 %all-gather.5.cloned.1.call-done = bf16[1024,512]{0,1:T(8,128)(2,1)} async-done(((bf16[1024,128]{0,1:T(8,128)(2,1)}), bf16[1024,512]{0,1:T(8,128)(2,1)}) %all-gather.5.cloned.1.call-update) | async-done | bytes 1048592 | tf_op jit(solution)/shard_map/all_gather | solution.py:23
  39.6 1.3 %collective-permute-start = (bf16[1024,512]{0,1:T(8,128)(2,1)}, bf16[1024,512]{0,1:T(8,128)(2,1)S(1)}, u32[]{:S(2)}, u32[]{:S(2)}) collective-permute-start(bf16[1024,512]{0,1:T(8,128)(2,1)} %all-gather.5.cloned.1.call-done), channel_id=1, source_target_pairs={{16,0},{17,1},{18,2},{19,3},{20,4},{21,5},{22,6},{23,7},{24,8},{25... | collective-permute-start | bytes 3145736 | tf_op jit(solution)/shard_map/ppermute | solution.py:10
  40.9 3.4 %collective-permute-done = bf16[1024,512]{0,1:T(8,128)(2,1)S(1)} collective-permute-done((bf16[1024,512]{0,1:T(8,128)(2,1)}, bf16[1024,512]{0,1:T(8,128)(2,1)S(1)}, u32[]{:S(2)}, u32[]{:S(2)}) %collective-permute-start) | collective-permute-done | bytes 1048608 | tf_op jit(solution)/shard_map/ppermute | solution.py:10
  44.4 2.2 %fusion = bf16[1024,512]{0,1:T(8,128)(2,1)S(1)} fusion(s32[]{:T(128)S(6)} %select_n.12, bf16[1024,512]{0,1:T(8,128)(2,1)} %all-gather.5.cloned.1.call-done, bf16[1024,512]{0,1:T(8,128)(2,1)S(1)} %collective-permute-done), kind=kLoop, calls=%fused_computation.3 | loop fusion | flops 2097152 | bytes 3145732 | tf_op jit(solution)/shard_map/concatenate | solution.py:27
  46.6 0.4 convolution_bitcast_fusion
  47.1 0.8 copy.18
  47.9 0.0 all-gather.7.cloned.1.call-update
  47.9 0.0 reduce-scatter.2.cloned.1.call-start
  48.0 0.1 copy.20
  48.1 13.9 %all_gather.19 = bf16[256,512]{0,1:T(8,128)(2,1)S(1)} all-gather(bf16[256,128]{0,1:T(8,128)(2,1)S(1)} %copy.20), channel_id=1, replica_groups=mesh['row'=2,'col'=4,'ind'=4] {'col'}, dimensions={1}, use_global_device_ids=true | all-gather | bytes 327680 | tf_op jit(solution)/shard_map/all_gather | solution.py:24
  62.0 1.3 %collective-permute-start.1 = (bf16[256,512]{0,1:T(8,128)(2,1)S(1)}, bf16[256,512]{0,1:T(8,128)(2,1)S(1)}, u32[]{:S(2)}, u32[]{:S(2)}) collective-permute-start(bf16[256,512]{0,1:T(8,128)(2,1)S(1)} %all_gather.19), channel_id=1, source_target_pairs={{16,0},{17,1},{18,2},{19,3},{20,4},{21,5},{22,6},{23,7},{24,8},{25... | collective-permute-start | bytes 786440 | tf_op jit(solution)/shard_map/ppermute | solution.py:10
  63.3 9.2 %all-gather.1 = s32[4,1,128]{2,1,0:T(1,128)S(1)} all-gather(s32[1,1,128]{2,1,0:T(1,128)S(1)} %bitcast.28), channel_id=1, replica_groups=mesh['row'=2,'col'=4,'ind'=4] {'col'}, dimensions={0}, use_global_device_ids=true | all-gather | bytes 2560 | tf_op jit(solution)/shard_map/all_gather | solution.py:21
  72.4 0.1 iota_add_fusion
  72.5 0.1 iota_add_fusion.1
  72.6 1.2 %all-gather.7.cloned.1.call-done = f32[16,128,128]{2,1,0:T(8,128)} async-done(((f32[4,128,128]{2,1,0:T(8,128)}), f32[16,128,128]{2,1,0:T(8,128)}) %all-gather.7.cloned.1.call-update) | async-done | bytes 1048592 | tf_op jit(solution)/shard_map/all_gather | solution.py:34
  73.8 1.3 %reduce_sum.9 = f32[4,128,128]{2,1,0:T(8,128)S(1)} reduce(f32[4,4,128,128]{3,2,1,0:T(8,128)} %bitcast.24, f32[]{:T(128)} %constant.49.clone.1), dimensions={0}, to_apply=%region_1.2 | reduce | flops 196608 | bytes 1310724 | tf_op jit(solution)/shard_map/reduce_sum | solution.py:34
  75.1 0.1 copy.30
  75.2 0.3 fusion.3
  75.5 0.2 copy.22
  75.7 0.1 broadcast_in_dim.11
  75.8 0.1 constant_dynamic-update-slice_fusion
  75.9 1.6 %collective-permute-start.2 = (f32[256,512]{1,0:T(8,128)S(1)}, f32[256,512]{1,0:T(8,128)S(1)}, u32[]{:S(2)}, u32[]{:S(2)}) collective-permute-start(f32[256,512]{1,0:T(8,128)S(1)} %slice.29), channel_id=1, source_target_pairs={{0,16},{1,17},{2,18},{3,19},{4,20},{5,21},{6,22},{7,23},{8,24},{9,... | collective-permute-start | bytes 1572872 | tf_op jit(solution)/shard_map/ppermute | solution.py:10
  77.5 0.6 compare_reduce_fusion
  78.2 0.6 fusion.2
  78.8 0.4 fusion.4
  79.2 0.2 copy.25
  79.4 1.6 %fusion.1 = f32[256,512]{1,0:T(8,128)} fusion(f32[256,512]{1,0:T(8,128)S(1)} %collective-permute-done.2, f32[256,512]{1,0:T(8,128)S(1)} %copy.25, f32[256,1024]{1,0:T(8,128)S(1)} %constant_dynamic-update-slice_fusion, pred[]{:T(512)} %compare_reduce_fusion), kind=kLoop, calls=%fused_computation.5 | loop fusion | flops 393216 | bytes 2097153 | tf_op jit(solution)/shard_map/add | solution.py:57
  81.0 0.0 reduce-scatter.2.cloned.1.call-update
  81.0 22.0 %reduce-scatter.2.cloned.1.call-done = f32[256,128]{1,0:T(8,128)} async-done(((f32[256,512]{1,0:T(8,128)}), f32[256,128]{1,0:T(8,128)}) %reduce-scatter.2.cloned.1.call-update) | async-done | bytes 131088 | tf_op jit(solution)/shard_map/reduce_scatter | solution.py:58
  (11 shorter events, 0.1 us)
Async XLA Ops:
  6.5 33.1 %all-gather.5.cloned.1.call-start = ((), (), s32[]{:S(2)}) async-start(), calls=%async_computation.1 | async-start | bytes 1310720 | tf_op jit(solution)/shard_map/all_gather | solution.py:23
  8.4 65.4 %all-gather.7.cloned.1.call-start = ((), (), s32[]{:S(2)}) async-start(), calls=%async_computation.3 | async-start | bytes 1310720 | tf_op jit(solution)/shard_map/all_gather | solution.py:34
  39.6 4.8 %collective-permute-start = (bf16[1024,512]{0,1:T(8,128)(2,1)}, bf16[1024,512]{0,1:T(8,128)(2,1)S(1)}, u32[]{:S(2)}, u32[]{:S(2)}) collective-permute-start(bf16[1024,512]{0,1:T(8,128)(2,1)} %all-gather.5.cloned.1.call-done), channel_id=1, source_target_pairs={{16,0},{17,1},{18,2},{19,3},{20,4},{21,5},{22,6},{23,7},{24,8},{25... | collective-permute-start | bytes 3145736 | tf_op jit(solution)/shard_map/ppermute | solution.py:10
  40.9 5.7 %copy-start = (bf16[1024,512]{0,1:T(8,128)(2,1)S(1)}, bf16[1024,512]{0,1:T(8,128)(2,1)}, u32[]{:S(2)}) copy-start(bf16[1024,512]{0,1:T(8,128)(2,1)} %all-gather.5.cloned.1.call-done) | copy-start | bytes 3145732
  46.6 1.4 %copy-start.1 = (bf16[256,128]{1,0:T(8,128)(2,1)S(1)}, bf16[256,128]{1,0:T(8,128)(2,1)}, u32[]{:S(2)}) copy-start(bf16[256,128]{1,0:T(8,128)(2,1)} %param.6) | copy-start | bytes 196612
  47.1 16.2 %copy-start.2 = (s32[128]{0:T(128)S(1)}, s32[128]{0:T(128)}, u32[]{:S(2)}) copy-start(s32[128]{0:T(128)} %param.7) | copy-start | bytes 1540
  47.9 55.1 %reduce-scatter.2.cloned.1.call-start = ((), (), s32[]{:S(2)}) async-start(), calls=%async_computation.2 | async-start | bytes 655360 | tf_op jit(solution)/shard_map/reduce_scatter | solution.py:58
  62.0 16.2 %collective-permute-start.1 = (bf16[256,512]{0,1:T(8,128)(2,1)S(1)}, bf16[256,512]{0,1:T(8,128)(2,1)S(1)}, u32[]{:S(2)}, u32[]{:S(2)}) collective-permute-start(bf16[256,512]{0,1:T(8,128)(2,1)S(1)} %all_gather.19), channel_id=1, source_target_pairs={{16,0},{17,1},{18,2},{19,3},{20,4},{21,5},{22,6},{23,7},{24,8},{25... | collective-permute-start | bytes 786440 | tf_op jit(solution)/shard_map/ppermute | solution.py:10
  75.9 3.5 %collective-permute-start.2 = (f32[256,512]{1,0:T(8,128)S(1)}, f32[256,512]{1,0:T(8,128)S(1)}, u32[]{:S(2)}, u32[]{:S(2)}) collective-permute-start(f32[256,512]{1,0:T(8,128)S(1)} %slice.29), channel_id=1, source_target_pairs={{0,16},{1,17},{2,18},{3,19},{4,20},{5,21},{6,22},{7,23},{8,24},{9,... | collective-permute-start | bytes 1572872 | tf_op jit(solution)/shard_map/ppermute | solution.py:10
Sparse Core Ops, SparseCore 0:
  8.9 30.6 all-gather.4
  48.1 25.6 all-gather.6
  81.1 21.8 reduce-scatter.1
